TPU v7x, 32 devices: a whole 2x2x4 slice. The times are simulated.
32 devices in a mesh: dp: 16 (over z, y, core), tensor: 2 (over x).
Axes of the slice: x: 2, y: 2, z: 4, core: 2. Of those that a mesh axis runs over, the one named last changes fastest.
Arguments:
- queries: bfloat16 [16, 64, 64, 128], P('dp', None, 'tensor'), may hold values from -6 to 6
- tree_keys: bfloat16 [16, 64, 8, 128], P('dp', None, 'tensor'), may hold values from -6 to 6
- tree_values: bfloat16 [16, 64, 8, 128], P('dp', None, 'tensor'), may hold values from -6 to 6
- cache_keys: bfloat16 [16, 8192, 8, 128], P('dp', None, 'tensor'), may hold values from -6 to 6
- cache_values: bfloat16 [16, 8192, 8, 128], P('dp', None, 'tensor'), may hold values from -6 to 6
- cache_len: int32 [16], P('dp'), may hold values from 1024 to 8192, as said below
- tree_parent: int32 [16, 64], P('dp'), may hold values from -1 to 62, as said below
- path_nodes: int32 [16, 8], P('dp'), may hold values from 0 to 63, as said below
- path_len: int32 [16], P('dp'), may hold values from 1 to 8, as said below
- out_weight: bfloat16 [8192, 8192], P('tensor', 'dp'), may hold values from -1 to 1
- norm_gain: float32 [8192], P('dp'), may hold values from 0.5 to 1.5
Outputs:
- verify_out: bfloat16 [16, 64, 8192], P('dp', None, 'tensor')
- paths_hidden: bfloat16 [128, 8192], P('tensor', 'dp')
Inputs may be any that keep to these rules, and one draw needn't show every extreme that they name: `cache_len`: some row has exactly 8192. tree_parent[r, 0] = -1 marks the root; every other token's parent has a lower index. path_nodes[r, 0] = 0, and for 0 < k < path_len[r] path_nodes[r, k] is a child of path_nodes[r, k - 1]; slots k >= path_len[r] hold 0. `path_len`: some row has the full 8.
All inputs are finite; a program needn't handle non-finite values.
Results may differ from a plain program's by a relative error of at most 0.015.
Values may be sent and summed in bfloat16 or wider, within the bound.
No kernel may reach another device: no remote copies, remote signals or barrier semaphores. Data moves between devices by JAX's collectives and lax.ppermute only.
A program may use at most 192 MiB of HBM per device.

v0:
```python
import math

import jax
import jax.numpy as jnp
from jax import lax
from jax.sharding import PartitionSpec as P

D = 8192


NEG_FILL = -1e30
EPSILON = 1e-05


def ancestor_table(tree_parent):
    tree_size = tree_parent.shape[-1]
    node_ids = jnp.arange(tree_size, dtype=jnp.int32)
    parent_hot = (tree_parent[:, :, None] == node_ids[None, None, :]).astype(jnp.float32)
    reachable = parent_hot + jnp.eye(tree_size, dtype=jnp.float32)[None]
    for squaring in range(max(1, (tree_size - 1).bit_length())):
        reachable = jnp.minimum(
            jnp.einsum("rij,rjk->rik", reachable, reachable, precision=lax.Precision.HIGHEST), 1.0
        )
    return reachable > 0.5


def attend(query_rows, allowed, tree_keys, tree_values, cache_keys, cache_values, cache_len):
    row_count, query_len, local_heads, head_dim = query_rows.shape
    cache_size, kv_local = (cache_keys.shape[1], cache_keys.shape[2])
    groups = local_heads // kv_local
    grouped = query_rows.reshape(row_count, query_len, kv_local, groups, head_dim)
    score_scale = 1.0 / math.sqrt(head_dim)
    block_len = min(cache_size, 2048)

    def absorb(state, key_block, value_block, permitted):
        running_max, running_sum, running_out = state
        scores = (
            jnp.einsum("rqkgd,rckd->rqkgc", grouped, key_block, preferred_element_type=jnp.float32)
            * score_scale
        )
        mask_full = permitted[:, :, None, None, :]
        scores = jnp.where(mask_full, scores, NEG_FILL)
        new_max = jnp.maximum(running_max, jnp.max(scores, axis=-1))
        weights = jnp.where(mask_full, jnp.exp(scores - new_max[..., None]), 0.0)
        rescale = jnp.exp(running_max - new_max)
        new_sum = running_sum * rescale + jnp.sum(weights, axis=-1)
        update = jnp.einsum(
            "rqkgc,rckd->rqkgd",
            weights.astype(jnp.bfloat16),
            value_block,
            preferred_element_type=jnp.float32,
        )
        new_out = running_out * rescale[..., None] + update
        return (new_max, new_sum, new_out)

    state = (
        jnp.full((row_count, query_len, kv_local, groups), NEG_FILL, jnp.float32),
        jnp.zeros((row_count, query_len, kv_local, groups), jnp.float32),
        jnp.zeros((row_count, query_len, kv_local, groups, head_dim), jnp.float32),
    )
    positions = jnp.arange(block_len, dtype=jnp.int32)
    for block_index in range(cache_size // block_len):
        offset = block_index * block_len
        key_block = cache_keys[:, offset : offset + block_len]
        value_block = cache_values[:, offset : offset + block_len]
        permitted = (offset + positions)[None, None, :] < cache_len[:, None, None]
        permitted = jnp.broadcast_to(permitted, (row_count, query_len, block_len))
        state = absorb(state, key_block, value_block, permitted)
    state = absorb(state, tree_keys, tree_values, allowed)
    attended = state[2] / state[1][..., None]
    return attended.reshape(row_count, query_len, local_heads * head_dim).astype(jnp.bfloat16)


def shards(
    queries,
    tree_keys,
    tree_values,
    cache_keys,
    cache_values,
    cache_len,
    tree_parent,
    path_nodes,
    path_len,
    out_weight,
    norm_gain,
):
    allowed = ancestor_table(tree_parent)
    slot_ids = jnp.arange(path_nodes.shape[1], dtype=jnp.int32)
    slot_live = slot_ids[None, :] < path_len[:, None]
    path_queries = jnp.take_along_axis(queries, path_nodes[:, :, None, None], axis=1)
    path_allowed = jnp.take_along_axis(allowed, path_nodes[:, :, None], axis=1)
    picked = attend(
        path_queries, path_allowed, tree_keys, tree_values, cache_keys, cache_values, cache_len
    )
    picked = jnp.where(slot_live[:, :, None], picked, jnp.zeros((), jnp.bfloat16))
    path_rows = picked.reshape(-1, picked.shape[-1])
    projected = jnp.dot(
        lax.all_gather(path_rows, "dp", axis=0, tiled=True),
        out_weight,
        preferred_element_type=jnp.float32,
    )
    verify_out = attend(
        queries, allowed, tree_keys, tree_values, cache_keys, cache_values, cache_len
    )
    local_tokens = projected.shape[0] // lax.axis_size("tensor")
    summed = lax.psum(projected.astype(jnp.bfloat16), "tensor").astype(jnp.float32)
    squares = lax.psum(jnp.sum(summed * summed, axis=1), "dp")
    inverse = lax.rsqrt(squares / D + EPSILON)
    normed = summed * inverse[:, None] * norm_gain[None, :]
    first_token = lax.axis_index("tensor") * local_tokens
    paths_hidden = lax.dynamic_slice_in_dim(normed, first_token, local_tokens, 0).astype(
        jnp.bfloat16
    )
    return (verify_out, paths_hidden)


def solution(mesh):
    return jax.shard_map(
        shards,
        mesh=mesh,
        in_specs=(
            P("dp", None, "tensor", None),
            P("dp", None, "tensor", None),
            P("dp", None, "tensor", None),
            P("dp", None, "tensor", None),
            P("dp", None, "tensor", None),
            P("dp"),
            P("dp", None),
            P("dp", None),
            P("dp"),
            P("tensor", "dp"),
            P("dp"),
        ),
        out_specs=(P("dp", None, "tensor"), P("tensor", "dp")),
        check_vma=False,
    )
```

profile of v0, /device:TPU:0, one launch (start us, length us, event | category | flops | bytes accessed | tf_op | source)
XLA Modules:
  0.0 206.6 jit_solution(12453992787118050697)
XLA Ops:
  9.3 6.4 %fusion.158 = (bf16[1,2048,4,128]{3,2,1,0:T(4,128)(2,1)}, bf16[1,2048,4,128]{3,2,1,0:T(4,128)(2,1)}, bf16[1,2048,4,128]{3,2,1,0:T(4,128)(2,1)S(1)}, bf16[1,2048,4,128]{3,2,1,0:T(4,128)(2,1)}) fusion(bf16[1,8192,4,128]{3,2,1,0:T(4,128)(2,1)} %param.14), kind=kLoop, calls=%fused_computation.225 | loop fusion | bytes 16777216 | tf_op jit(solution)/shard_map/slice | solution.py:64
  18.0 5.2 %fusion.157 = (bf16[1,2048,4,128]{3,2,1,0:T(4,128)(2,1)S(1)}, bf16[1,2048,4,128]{3,2,1,0:T(4,128)(2,1)S(1)}, bf16[1,2048,4,128]{3,2,1,0:T(4,128)(2,1)S(1)}, bf16[1,2048,4,128]{3,2,1,0:T(4,128)(2,1)S(1)}) fusion(bf16[1,8192,4,128]{3,2,1,0:T(4,128)(2,1)} %param.15), kind=kLoop, calls=%fused_computation.224 | loop fusion | bytes 16777216 | tf_op jit(solution)/shard_map/slice | solution.py:65
  24.4 2.2 %copy-done.5 = bf16[1,2048,4,128]{3,2,1,0:T(4,128)(2,1)S(1)} copy-done((bf16[1,2048,4,128]{3,2,1,0:T(4,128)(2,1)S(1)}, bf16[1,2048,4,128]{3,2,1,0:T(4,128)(2,1)}, u32[]{:S(2)}) %copy-start.5) | copy-done | bytes 2097176
  29.3 1.0 fusion.163
  37.7 9.6 %bitcast_reduce_fusion.3 = (f32[64,4,8]{0,2,1:T(8,128)S(1)}, f32[4,2048,64,8]{1,2,3,0:T(8,128)}) fusion(pred[2048]{0:T(1024)(128)(4,1)S(1)} %get-tuple-element.57, bf16[64,4,8,128]{3,2,1,0:T(8,128)(2,1)S(1)} %bitcast.449, bf16[1,2048,4,128]{3,2,1,0:T(4,128)(2,1)} %get-tuple-element.24), kind=kOutput, calls=%fused_computation.18 | convolution fusion | flops 1086322688 | bytes 19408896 | tf_op jit(solution)/shard_map/rqkgd,rckd->rqkgc/dot_general | solution.py:38
  47.3 7.3 %bitcast_reduce_fusion = (f32[64,4,8]{0,2,1:T(8,128)S(1)}, f32[4,2048,64,8]{1,2,3,0:T(8,128)}) fusion(pred[2048]{0:T(1024)(128)(4,1)S(1)} %get-tuple-element.54, bf16[64,4,8,128]{3,2,1,0:T(8,128)(2,1)S(1)} %bitcast.451, bf16[1,2048,4,128]{3,2,1,0:T(4,128)(2,1)S(1)} %copy-done.6), kind=kOutput, calls=%fused_computation.3 | convolution fusion | flops 1086322688 | bytes 19408896 | tf_op jit(solution)/shard_map/rqkgd,rckd->rqkgc/dot_general | solution.py:38
  54.6 7.3 %bitcast_reduce_fusion.1 = (f32[64,4,8]{0,2,1:T(8,128)S(1)}, f32[4,2048,64,8]{1,2,3,0:T(8,128)}) fusion(pred[2048]{0:T(1024)(128)(4,1)S(1)} %get-tuple-element.55, bf16[64,4,8,128]{3,2,1,0:T(8,128)(2,1)S(1)} %bitcast.452, bf16[1,2048,4,128]{3,2,1,0:T(4,128)(2,1)S(1)} %copy-done.4), kind=kOutput, calls=%fused_computation.8 | convolution fusion | flops 1086322688 | bytes 19408896 | tf_op jit(solution)/shard_map/rqkgd,rckd->rqkgc/dot_general | solution.py:38
  61.8 7.3 %bitcast_reduce_fusion.2 = (f32[64,4,8]{0,2,1:T(8,128)S(1)}, f32[4,2048,64,8]{1,2,3,0:T(8,128)}) fusion(pred[2048]{0:T(1024)(128)(4,1)S(1)} %get-tuple-element.56, bf16[64,4,8,128]{3,2,1,0:T(8,128)(2,1)S(1)} %bitcast.453, bf16[1,2048,4,128]{3,2,1,0:T(4,128)(2,1)S(1)} %get-tuple-element.26), kind=kOutput, calls=%fused_computation.13 | convolution fusion | flops 1086322688 | bytes 19408896 | tf_op jit(solution)/shard_map/rqkgd,rckd->rqkgc/dot_general | solution.py:38
  70.5 9.5 %fusion.10 = f32[64,4,8]{0,2,1:T(8,128)S(1)} fusion(f32[4,2048,64,8]{1,2,3,0:T(8,128)} %get-tuple-element.41, f32[64,4,8]{0,2,1:T(8,128)S(1)} %get-tuple-element.19, pred[2048]{0:T(1024)(128)(4,1)S(1)} %get-tuple-element.56), kind=kLoop, calls=%fused_computation.24 | loop fusion | flops 20969472 | bytes 16795648 | tf_op jit(solution)/shard_map/reduce_sum | solution.py:46
  80.0 1.3 copy-done.2
  81.3 6.2 %fusion.22 = f32[4,64,8,128]{3,1,2,0:T(8,128)} fusion(f32[4,2048,64,8]{1,2,3,0:T(8,128)S(1)} %copy-done.2, f32[64,4,8]{0,2,1:T(8,128)S(1)} %get-tuple-element.19, pred[2048]{0:T(1024)(128)(4,1)S(1)} %get-tuple-element.56, bf16[1,2048,4,128]{3,2,1,0:T(4,128)(2,1)} %copy-done.14), kind=kOutput, calls=%fused_computation.35 | convolution fusion | flops 1094713344 | bytes 19933184 | tf_op jit(solution)/shard_map/rqkgc,rckd->rqkgd/dot_general | solution.py:47
  87.5 9.8 %fusion.12 = f32[64,4,8]{0,2,1:T(8,128)S(1)} fusion(f32[4,2048,64,8]{1,2,3,0:T(8,128)} %get-tuple-element.39, f32[64,4,8]{0,2,1:T(8,128)S(1)} %get-tuple-element.18, pred[2048]{0:T(1024)(128)(4,1)S(1)} %get-tuple-element.55), kind=kLoop, calls=%fused_computation.26 | loop fusion | flops 20969472 | bytes 16795648 | tf_op jit(solution)/shard_map/reduce_sum | solution.py:46
  97.3 8.6 %fusion.24 = f32[4,64,8,128]{3,1,2,0:T(8,128)} fusion(f32[4,2048,64,8]{1,2,3,0:T(8,128)} %get-tuple-element.39, f32[64,4,8]{0,2,1:T(8,128)S(1)} %get-tuple-element.18, pred[2048]{0:T(1024)(128)(4,1)S(1)} %get-tuple-element.55, bf16[1,2048,4,128]{3,2,1,0:T(4,128)(2,1)S(1)} %copy-done.13), kind=kOutput, calls=%fused_computation.36 | convolution fusion | flops 1094713344 | bytes 19933184 | tf_op jit(solution)/shard_map/rqkgc,rckd->rqkgd/dot_general | solution.py:47
  105.9 4.4 %fusion.14 = f32[64,4,8]{0,2,1:T(8,128)S(1)} fusion(f32[4,2048,64,8]{1,2,3,0:T(8,128)S(1)} %bitcast.458, f32[64,4,8]{0,2,1:T(8,128)S(1)} %get-tuple-element.17, pred[2048]{0:T(1024)(128)(4,1)S(1)} %get-tuple-element.54), kind=kLoop, calls=%fused_computation.28 | loop fusion | flops 20969472 | bytes 16795648 | tf_op jit(solution)/shard_map/reduce_sum | solution.py:46
  110.4 8.6 %fusion.26 = f32[4,64,8,128]{3,1,2,0:T(8,128)} fusion(f32[4,2048,64,8]{1,2,3,0:T(8,128)} %get-tuple-element.37, f32[64,4,8]{0,2,1:T(8,128)S(1)} %get-tuple-element.17, pred[2048]{0:T(1024)(128)(4,1)S(1)} %get-tuple-element.54, bf16[1,2048,4,128]{3,2,1,0:T(4,128)(2,1)S(1)} %copy-done.11), kind=kOutput, calls=%fused_computation.37 | convolution fusion | flops 1094713344 | bytes 19933184 | tf_op jit(solution)/shard_map/rqkgc,rckd->rqkgd/dot_general | solution.py:47
  119.0 4.4 %fusion.8 = f32[64,4,8]{0,2,1:T(8,128)S(1)} fusion(f32[4,2048,64,8]{1,2,3,0:T(8,128)S(1)} %bitcast.456, f32[64,4,8]{0,2,1:T(8,128)S(1)} %get-tuple-element.33, pred[2048]{0:T(1024)(128)(4,1)S(1)} %get-tuple-element.57), kind=kLoop, calls=%fused_computation.22 | loop fusion | flops 20969472 | bytes 16795648 | tf_op jit(solution)/shard_map/reduce_sum | solution.py:46
  125.9 1.5 copy.45
  127.4 8.4 %fusion.20 = f32[4,64,8,128]{3,1,2,0:T(8,128)} fusion(f32[4,2048,64,8]{1,2,3,0:T(8,128)} %get-tuple-element.43, f32[64,4,8]{0,2,1:T(8,128)} %copy-done.18, pred[2048]{0:T(1024)(128)(4,1)S(1)} %get-tuple-element.57, bf16[1,2048,4,128]{3,2,1,0:T(4,128)(2,1)S(1)} %copy-done.9), kind=kOutput, calls=%fused_computation.34 | convolution fusion | flops 1094713344 | bytes 19933184 | tf_op jit(solution)/shard_map/rqkgc,rckd->rqkgd/dot_general | solution.py:47
  135.9 4.0 %convolution_convert_fusion = bf16[128,512]{1,0:T(8,128)(2,1)} fusion(bf16[128,4096]{1,0:T(8,128)(2,1)} %all-gather.2.cloned.1.call-done, bf16[4096,512]{1,0:T(8,128)(2,1)} %param.20), kind=kOutput, calls=%fused_computation.97 | convolution fusion | flops 536936448 | bytes 5373952 | tf_op jit(solution)/shard_map/dot_general | solution.py:97
  140.0 4.8 %fusion.67 = bf16[1,64,4,8,128]{4,3,1,2,0:T(8,128)(2,1)S(1)} fusion(bf16[64,4,8,64]{3,2,0,1:T(8,128)(2,1)S(1)} %copy.67, f32[4,64,8,128]{3,1,2,0:T(8,128)} %fusion.26, f32[4,64,8,128]{3,1,2,0:T(8,128)} %fusion.24, f32[4,64,8,128]{3,1,2,0:T(8,128)S(1)} %copy-done.24, f32[4,64,8,128]{3,1,2,0:T(8,128)} %fusion.20, f32[64,4,8]{2,0,1:T(8,128)S(1)} %copy-done.16, ...), kind=kOutput, calls=%fused_computation.95 | convolution fusion | flops 36438016 | bytes 5095424 | tf_op jit(solution)/shard_map/rqkgc,rckd->rqkgd/dot_general | solution.py:47
  144.9 1.0 convert_element_type.117
  145.9 18.4 %all-reduce.2.cloned.1.call-done = bf16[128,512]{1,0:T(8,128)(2,1)} async-done(((bf16[128,512]{1,0:T(8,128)(2,1)}), bf16[128,512]{1,0:T(8,128)(2,1)}) %all-reduce.2.cloned.1.call-update) | async-done | bytes 131088 | tf_op jit(solution)/shard_map/psum | solution.py:106
  164.3 1.0 multiply_reduce_fusion
  165.3 32.7 %psum.15 = f32[128]{0:T(128)S(1)} all-reduce(f32[128]{0:T(128)S(1)} %multiply_reduce_fusion), channel_id=1, replica_groups=mesh['dp'=16,'tensor'=2] {'dp'}, use_global_device_ids=true, to_apply=%region_22.23 | all-reduce | flops 128 | bytes 1024 | tf_op jit(solution)/shard_map/psum | solution.py:107
  (122 shorter events, 19.9 us)
Async XLA Ops:
  7.2 9.7 %copy-start = (bf16[1,64,32,128]{3,2,1,0:T(8,128)(2,1)S(1)}, bf16[1,64,32,128]{3,2,1,0:T(8,128)(2,1)}, u32[]{:S(2)}) copy-start(bf16[1,64,32,128]{3,2,1,0:T(8,128)(2,1)} %param.11) | copy-start | bytes 1572868
  7.2 128.7 %all-gather.2.cloned.1.call-start = ((), (), s32[]{:S(2)}) async-start(), calls=%async_computation | async-start | bytes 1114112 | tf_op jit(solution)/shard_map/all_gather | solution.py:98
  9.3 6.4 %copy-start.21 = (s32[1,64]{1,0:T(1,128)S(1)}, s32[1,64]{1,0:T(1,128)}, u32[]{:S(2)}) copy-start(s32[1,64]{1,0:T(1,128)} %param.17) | copy-start | bytes 772
  18.0 5.4 %copy-start.7 = (bf16[1,2048,4,128]{3,2,1,0:T(4,128)(2,1)S(1)}, bf16[1,2048,4,128]{3,2,1,0:T(4,128)(2,1)}, u32[]{:S(2)}) copy-start(bf16[1,2048,4,128]{3,2,1,0:T(4,128)(2,1)} %get-tuple-element.24) | copy-start | bytes 6291460
  23.3 7.8 %copy-start.10 = (bf16[1,2048,4,128]{3,2,1,0:T(4,128)(2,1)}, bf16[1,2048,4,128]{3,2,1,0:T(4,128)(2,1)S(1)}, u32[]{:S(2)}) copy-start(bf16[1,2048,4,128]{3,2,1,0:T(4,128)(2,1)S(1)} %get-tuple-element.23) | copy-start | bytes 6291460
  23.3 9.0 %copy-start.12 = (bf16[1,2048,4,128]{3,2,1,0:T(4,128)(2,1)}, bf16[1,2048,4,128]{3,2,1,0:T(4,128)(2,1)S(1)}, u32[]{:S(2)}) copy-start(bf16[1,2048,4,128]{3,2,1,0:T(4,128)(2,1)S(1)} %get-tuple-element.21) | copy-start | bytes 6291460
  23.3 10.2 %copy-start.14 = (bf16[1,2048,4,128]{3,2,1,0:T(4,128)(2,1)}, bf16[1,2048,4,128]{3,2,1,0:T(4,128)(2,1)S(1)}, u32[]{:S(2)}) copy-start(bf16[1,2048,4,128]{3,2,1,0:T(4,128)(2,1)S(1)} %get-tuple-element.22) | copy-start | bytes 6291460
  23.3 11.6 %copy-start.8 = (bf16[1,2048,4,128]{3,2,1,0:T(4,128)(2,1)}, bf16[1,2048,4,128]{3,2,1,0:T(4,128)(2,1)S(1)}, u32[]{:S(2)}) copy-start(bf16[1,2048,4,128]{3,2,1,0:T(4,128)(2,1)S(1)} %get-tuple-element.20) | copy-start | bytes 6291460
  37.4 126.8 %all-reduce.2.cloned.1.call-start = ((), (), s32[]{:S(2)}) async-start(), calls=%async_computation.1 | async-start | bytes 262144 | tf_op jit(solution)/shard_map/psum | solution.py:106
  37.7 9.6 %copy-start.6 = (bf16[1,2048,4,128]{3,2,1,0:T(4,128)(2,1)S(1)}, bf16[1,2048,4,128]{3,2,1,0:T(4,128)(2,1)}, u32[]{:S(2)}) copy-start(bf16[1,2048,4,128]{3,2,1,0:T(4,128)(2,1)} %get-tuple-element.27) | copy-start | bytes 6291460
  47.2 7.3 %copy-start.4 = (bf16[1,2048,4,128]{3,2,1,0:T(4,128)(2,1)S(1)}, bf16[1,2048,4,128]{3,2,1,0:T(4,128)(2,1)}, u32[]{:S(2)}) copy-start(bf16[1,2048,4,128]{3,2,1,0:T(4,128)(2,1)} %get-tuple-element.25) | copy-start | bytes 6291460
  70.5 48.5 %copy-start.18 = (f32[64,4,8]{0,2,1:T(8,128)}, f32[64,4,8]{0,2,1:T(8,128)S(1)}, u32[]{:S(2)}) copy-start(f32[64,4,8]{0,2,1:T(8,128)S(1)} %get-tuple-element.33) | copy-start | bytes 24580
  70.5 10.8 %copy-start.2 = (f32[4,2048,64,8]{1,2,3,0:T(8,128)S(1)}, f32[4,2048,64,8]{1,2,3,0:T(8,128)}, u32[]{:S(2)}) copy-start(f32[4,2048,64,8]{1,2,3,0:T(8,128)} %get-tuple-element.41) | copy-start | bytes 50331652
  87.5 9.8 %copy-start.13 = (bf16[1,2048,4,128]{3,2,1,0:T(4,128)(2,1)S(1)}, bf16[1,2048,4,128]{3,2,1,0:T(4,128)(2,1)}, u32[]{:S(2)}) copy-start(bf16[1,2048,4,128]{3,2,1,0:T(4,128)(2,1)} %copy-done.12) | copy-start | bytes 6291460
  87.5 18.4 %slice-start.4 = ((s8[16777216]{0:T(1024)(128)(4,1)}), s8[4194304]{0:T(1024)(128)(4,1)S(1)}, s32[]{:S(2)}) async-start(s8[16777216]{0:T(1024)(128)(4,1)} %bitcast.457), calls=%async_computation.6 | async-start | bytes 8388608
  87.5 18.4 %slice-start.5 = ((s8[16777216]{0:T(1024)(128)(4,1)}), s8[4194304]{0:T(1024)(128)(4,1)S(1)}, s32[]{:S(2)}) async-start(s8[16777216]{0:T(1024)(128)(4,1)} %bitcast.457), calls=%async_computation.7 | async-start | bytes 8388608
  97.3 8.6 %slice-start.6 = ((s8[16777216]{0:T(1024)(128)(4,1)}), s8[4194304]{0:T(1024)(128)(4,1)S(1)}, s32[]{:S(2)}) async-start(s8[16777216]{0:T(1024)(128)(4,1)} %bitcast.457), calls=%async_computation.8 | async-start | bytes 8388608
  97.3 8.6 %slice-start.7 = ((s8[16777216]{0:T(1024)(128)(4,1)}), s8[4194304]{0:T(1024)(128)(4,1)S(1)}, s32[]{:S(2)}) async-start(s8[16777216]{0:T(1024)(128)(4,1)} %bitcast.457), calls=%async_computation.9 | async-start | bytes 8388608
  105.9 13.1 %slice-start = ((s8[16777216]{0:T(1024)(128)(4,1)}), s8[4194304]{0:T(1024)(128)(4,1)S(1)}, s32[]{:S(2)}) async-start(s8[16777216]{0:T(1024)(128)(4,1)} %bitcast.455), calls=%async_computation.2 | async-start | bytes 8388608
  105.9 13.1 %slice-start.1 = ((s8[16777216]{0:T(1024)(128)(4,1)}), s8[4194304]{0:T(1024)(128)(4,1)S(1)}, s32[]{:S(2)}) async-start(s8[16777216]{0:T(1024)(128)(4,1)} %bitcast.455), calls=%async_computation.3 | async-start | bytes 8388608
  110.4 8.6 %slice-start.2 = ((s8[16777216]{0:T(1024)(128)(4,1)}), s8[4194304]{0:T(1024)(128)(4,1)S(1)}, s32[]{:S(2)}) async-start(s8[16777216]{0:T(1024)(128)(4,1)} %bitcast.455), calls=%async_computation.4 | async-start | bytes 8388608
  110.4 8.6 %slice-start.3 = ((s8[16777216]{0:T(1024)(128)(4,1)}), s8[4194304]{0:T(1024)(128)(4,1)S(1)}, s32[]{:S(2)}) async-start(s8[16777216]{0:T(1024)(128)(4,1)} %bitcast.455), calls=%async_computation.5 | async-start | bytes 8388608
  140.0 59.8 %copy-start.1 = (bf16[1,64,32,128]{3,2,1,0:T(8,128)(2,1)S(1)}, bf16[1,64,32,128]{3,2,1,0:T(8,128)(2,1)}, u32[]{:S(2)}) copy-start(bf16[1,64,32,128]{3,2,1,0:T(8,128)(2,1)} %param.11) | copy-start | bytes 1572868
  144.7 54.3 %copy-start.20 = (f32[512]{0:T(512)S(1)}, f32[512]{0:T(512)}, u32[]{:S(2)}) copy-start(f32[512]{0:T(512)} %param.21) | copy-start | bytes 6148
  (11 other events, 35.6 us)
Sparse Core Ops, SparseCore 0:
  37.6 40.5 all-gather.1
  140.0 24.2 all-reduce.1
where the time goes:
time: 207 us
  matrix products  80.9 us (39%)
  other arithmetic  36.3 us (18%)
  blocking collectives  32.7 us (16%)
  local copies, waits for them, and re-layouts  22.1 us (11%)
  waiting for transfers between devices  18.5 us (9%)
  between operations  15.9 us (8%)
    dot_general x10, matrix products, absorb(): jnp.einsum('rqkgc,rckd->rqkgd', weights.astype(jnp.bfloat16), value_block...  39.7 us
    dot_general x10, matrix products, absorb(): jnp.einsum('rqkgd,rckd->rqkgc', grouped, key_block, preferred_element_typ...  36.2 us
    psum x1, blocking collectives, shards(): squares = lax.psum(jnp.sum(summed * summed, axis=1), 'dp')  32.7 us
    reduce_sum x10, other arithmetic, absorb(): new_sum = running_sum * rescale + jnp.sum(weights, axis=-1)  30.6 us
    psum x1, waiting for transfers between devices, shards(): lax.psum(projected.astype(jnp.bfloat16), 'tensor').astype(jnp.float32)  18.4 us
    slice x1, local copies, waits for them, and re-layouts, attend(): key_block = cache_keys[:, offset:offset + block_len]  6.4 us
    slice x1, local copies, waits for them, and re-layouts, attend(): value_block = cache_values[:, offset:offset + block_len]  5.24 us
    unnamed x66, local copies, waits for them, and re-layouts  4.46 us
  transfers between devices with their start and end apart: 2, of which 1 were waited for; matrix products, arithmetic and copies ran while one was open for 50% of the time, Pallas kernels for 0%

commit v1 on v0

v1 whole, which is shorter than its diff:
```python
import functools
import math

import jax
import jax.numpy as jnp
from jax import lax
from jax.experimental import pallas as pl
from jax.experimental.pallas import tpu as pltpu
from jax.sharding import PartitionSpec as P

EPSILON = 1e-05
NEG = -1e30
LIMIT = 2.0**100
F32 = jnp.float32
BF16 = jnp.bfloat16


def dot_nt(a, b):
    return lax.dot_general(a, b, (((1,), (1,)), ((), ())), preferred_element_type=F32)


def ancestors(parent_row):
    t = parent_row.shape[1]
    row = lax.broadcasted_iota(jnp.int32, (t, t), 0)
    col = lax.broadcasted_iota(jnp.int32, (t, t), 1)
    reach = jnp.where((parent_row == row) | (row == col), 1.0, 0.0)
    for _ in range(max(1, (t - 1).bit_length())):
        half = reach.astype(BF16)
        reach = jnp.minimum(jnp.dot(half, half, preferred_element_type=F32), 1.0)
    return reach.T > 0.5


def attention_kernel(
    lens,
    nodes,
    plen,
    parent_ref,
    q_ref,
    tk_ref,
    tv_ref,
    k_ref,
    v_ref,
    k_hbm,
    v_hbm,
    out_ref,
    path_ref,
    kf,
    vf,
    tf,
    p_ref,
    acc_ref,
    sh_ref,
    of,
    pf,
    kb,
    vb,
    sem,
    *,
    kvh,
    groups,
    tree,
    sub,
    slow,
    scale,
):
    n = pl.program_id(0)
    c = k_ref.shape[0] // kvh
    m = groups * tree
    hd = q_ref.shape[2]
    length = lens[0]

    def head_rows(ref, g, start, count):
        return ref[pl.ds(g + kvh * start, count, stride=kvh), :]

    def tree_values(g):
        value = tf[1, pl.ds(g, tree, stride=kvh), :].astype(BF16)
        return jnp.concatenate([value, jnp.ones((tree, hd), BF16)], axis=1)

    def tree_scores(g):
        keys = tf[0, pl.ds(g, tree, stride=kvh), :].astype(BF16)
        return dot_nt(q_ref[g], keys) * scale

    @pl.when(n == 0)
    def _():
        tf[0] = tk_ref[...].astype(F32)
        tf[1] = tv_ref[...].astype(F32)
        allowed = jnp.tile(ancestors(parent_ref[...]), (groups, 1))
        diag_row = lax.broadcasted_iota(jnp.int32, (m, tree), 0) % tree
        diag = diag_row == lax.broadcasted_iota(jnp.int32, (m, tree), 1)
        for g in range(kvh):
            s = tree_scores(g)
            shift = jnp.sum(jnp.where(diag, s, 0.0), axis=1, keepdims=True)
            sh_ref[g] = jnp.broadcast_to(shift, (m, 128))
            p = jnp.where(allowed, jnp.exp2(s - shift), 0.0).astype(BF16)
            acc_ref[g] = jnp.dot(p, tree_values(g), preferred_element_type=F32)

    @pl.when(n * c < length)
    def _():
        live = lax.broadcasted_iota(jnp.int32, (c, 128), 0) < length - n * c
        ones = jnp.where(live, 1.0, 0.0).astype(BF16)
        for i in range(c // sub):
            rows = slice(i * sub * kvh, (i + 1) * sub * kvh)
            kf[rows] = k_ref[rows].astype(F32)
        for i in range(c // sub):
            rows = slice(i * sub * kvh, (i + 1) * sub * kvh)
            vf[rows] = v_ref[rows].astype(F32)
        for g in range(kvh):
            q = q_ref[g]
            shift = sh_ref[g]
            for i in range(c // sub):
                s = dot_nt(q, head_rows(kf, g, i * sub, sub).astype(BF16))
                p = [jnp.exp2(s[:, a : a + 128] * scale - shift) for a in range(0, sub, 128)]
                p_ref[:, i * sub : (i + 1) * sub] = jnp.concatenate(p, axis=1).astype(BF16)
            value = jnp.where(live, head_rows(vf, g, 0, c), 0.0).astype(BF16)
            value = jnp.concatenate([value, ones], axis=1)
            acc_ref[g] += jnp.dot(p_ref[...], value, preferred_element_type=F32)

    @pl.when(n == pl.num_programs(0) - 1)
    def _():
        fits = jnp.max(jnp.where(acc_ref[:, :, hd:] < LIMIT, 0.0, 1.0)) < 0.5

        @pl.when(jnp.logical_not(fits))
        def _():
            allowed = jnp.tile(ancestors(parent_ref[...]), (groups, 1))
            for g in range(kvh):
                s = jnp.where(allowed, tree_scores(g), NEG)
                top = jnp.max(s, axis=1, keepdims=True)
                p = jnp.where(allowed, jnp.exp2(s - top), 0.0).astype(BF16)
                sh_ref[g] = jnp.broadcast_to(top, (m, 128))
                acc_ref[g] = jnp.dot(p, tree_values(g), preferred_element_type=F32)

            def step(i, carry):
                span = pl.ds(pl.multiple_of(i * slow * kvh, slow * kvh), slow * kvh)
                copies = (
                    pltpu.make_async_copy(k_hbm.at[span], kb, sem.at[0]),
                    pltpu.make_async_copy(v_hbm.at[span], vb, sem.at[1]),
                )
                for copy in copies:
                    copy.start()
                for copy in copies:
                    copy.wait()
                kf[: slow * kvh] = kb[...].astype(F32)
                vf[: slow * kvh] = vb[...].astype(F32)
                left = length - i * slow
                col = lax.broadcasted_iota(jnp.int32, (m, slow), 1) < left
                live = lax.broadcasted_iota(jnp.int32, (slow, 128), 0) < left
                ones = jnp.where(live, 1.0, 0.0).astype(BF16)
                for g in range(kvh):
                    s = dot_nt(q_ref[g], head_rows(kf, g, 0, slow).astype(BF16)) * scale
                    s = jnp.where(col, s, NEG)
                    old = sh_ref[g]
                    top = jnp.maximum(old, jnp.max(s, axis=1, keepdims=True))
                    shrink = jnp.exp2(old - top)
                    p = [jnp.exp2(s[:, a : a + 128] - top) for a in range(0, slow, 128)]
                    p = jnp.concatenate(p, axis=1).astype(BF16)
                    value = jnp.where(live, head_rows(vf, g, 0, slow), 0.0).astype(BF16)
                    value = jnp.concatenate([value, ones], axis=1)
                    acc_ref[g] = acc_ref[g] * jnp.concatenate([shrink, shrink], axis=1) + jnp.dot(
                        p, value, preferred_element_type=F32
                    )
                    sh_ref[g] = top
                return carry

            lax.fori_loop(0, pl.cdiv(length, slow), step, 0)

        for g in range(kvh):
            rows = acc_ref[g, :, :hd] / acc_ref[g, :, hd:]
            for h in range(groups):
                lanes = slice((g * groups + h) * hd, (g * groups + h + 1) * hd)
                part = rows[h * tree : (h + 1) * tree]
                out_ref[:, lanes] = part.astype(BF16)
                of[:, lanes] = part
        for k in range(path_ref.shape[0]):
            row = of[pl.ds(nodes[k], 1), :]
            pf[k : k + 1, :] = jnp.where(k < plen[0], row, 0.0)
        path_ref[...] = pf[...].astype(BF16)


def attention(queries, tree_keys, tree_values, cache_keys, cache_values, lens, parent, nodes, plen):
    tree, heads, hd = queries.shape[1:]
    size, kvh = cache_keys.shape[1:3]
    groups = heads // kvh
    depth = nodes.shape[1]
    m = groups * tree
    c = min(1024, size)
    sub = min(256, c)
    slow = sub
    q = queries[0].transpose(1, 0, 2).reshape(kvh, m, hd)
    flat = lambda x: x.reshape(-1, hd)
    kernel = functools.partial(
        attention_kernel,
        kvh=kvh,
        groups=groups,
        tree=tree,
        sub=sub,
        slow=slow,
        scale=math.log2(math.e) / math.sqrt(hd),
    )
    whole = lambda *shape: pl.BlockSpec(shape, lambda n, *_: (0,) * len(shape))

    def chunk(n, lens, *_):
        return (jnp.minimum(n, (lens[0] - 1) // c), 0)

    anywhere = pl.BlockSpec(memory_space=pl.ANY)
    return pl.pallas_call(
        kernel,
        grid_spec=pltpu.PrefetchScalarGridSpec(
            num_scalar_prefetch=3,
            grid=(size // c,),
            in_specs=[
                whole(1, tree),
                whole(kvh, m, hd),
                whole(tree * kvh, hd),
                whole(tree * kvh, hd),
                pl.BlockSpec((c * kvh, hd), chunk),
                pl.BlockSpec((c * kvh, hd), chunk),
                anywhere,
                anywhere,
            ],
            out_specs=[whole(tree, heads * hd), whole(depth, heads * hd)],
            scratch_shapes=[
                pltpu.VMEM((c * kvh, hd), F32),
                pltpu.VMEM((c * kvh, hd), F32),
                pltpu.VMEM((2, tree * kvh, hd), F32),
                pltpu.VMEM((m, c), BF16),
                pltpu.VMEM((kvh, m, 2 * hd), F32),
                pltpu.VMEM((kvh, m, 128), F32),
                pltpu.VMEM((tree, heads * hd), F32),
                pltpu.VMEM((depth, heads * hd), F32),
                pltpu.VMEM((slow * kvh, hd), BF16),
                pltpu.VMEM((slow * kvh, hd), BF16),
                pltpu.SemaphoreType.DMA((2,)),
            ],
        ),
        out_shape=[
            jax.ShapeDtypeStruct((tree, heads * hd), BF16),
            jax.ShapeDtypeStruct((depth, heads * hd), BF16),
        ],
        name="attention",
    )(
        lens,
        nodes.reshape(-1),
        plen,
        parent,
        q,
        flat(tree_keys),
        flat(tree_values),
        flat(cache_keys),
        flat(cache_values),
        flat(cache_keys),
        flat(cache_values),
    )


def swap(x, axis, bit):
    size = lax.axis_size(axis)
    return lax.ppermute(x, axis, [(i, i ^ bit) for i in range(size)])


def bits_down(size):
    return [1 << b for b in reversed(range((size - 1).bit_length()))]


def gather_xor(x, axis):
    order = [0]
    for bit in bits_down(lax.axis_size(axis)):
        x = jnp.concatenate([x, swap(x, axis, bit)], axis=0)
        order = order + [b ^ bit for b in order]
    return x, order


def shards(
    queries,
    tree_keys,
    tree_values,
    cache_keys,
    cache_values,
    cache_len,
    tree_parent,
    path_nodes,
    path_len,
    out_weight,
    norm_gain,
):
    verify, picked = attention(
        queries, tree_keys, tree_values, cache_keys, cache_values, cache_len, tree_parent, path_nodes, path_len
    )
    dp = lax.axis_size("dp")
    tensor = lax.axis_size("tensor")
    depth = path_nodes.shape[1]
    width = dp * out_weight.shape[1]
    rows, order = gather_xor(picked, "dp")
    projected = jnp.dot(rows, out_weight, preferred_element_type=F32)
    position = [0] * dp
    for at, block in enumerate(order):
        position[block] = at
    blocks = jnp.arange(dp, dtype=jnp.int32) ^ lax.axis_index("dp")
    projected = projected.reshape(dp, depth, -1)[jnp.asarray(position, jnp.int32)[blocks]]
    projected = projected.reshape(dp * depth, -1)
    tokens = dp * depth // tensor
    if tensor == 2:
        mine = lax.axis_index("tensor")
        away = lax.dynamic_slice_in_dim(projected, (1 - mine) * tokens, tokens, 0)
        kept = lax.dynamic_slice_in_dim(projected, mine * tokens, tokens, 0)
        summed = kept + swap(away.astype(BF16), "tensor", 1).astype(F32)
    else:
        summed = lax.psum_scatter(projected.astype(BF16), "tensor", tiled=True).astype(F32)
    squares = jnp.sum(summed * summed, axis=1)
    for bit in bits_down(dp):
        squares = squares + swap(squares, "dp", bit)
    inverse = lax.rsqrt(squares / width + EPSILON)
    hidden = summed * inverse[:, None] * norm_gain[None, :]
    return (verify[None], hidden.astype(BF16))


def solution(mesh):
    return jax.shard_map(
        shards,
        mesh=mesh,
        in_specs=(
            P("dp", None, "tensor", None),
            P("dp", None, "tensor", None),
            P("dp", None, "tensor", None),
            P("dp", None, "tensor", None),
            P("dp", None, "tensor", None),
            P("dp"),
            P("dp", None),
            P("dp", None),
            P("dp"),
            P("tensor", "dp"),
            P("dp"),
        ),
        out_specs=(P("dp", None, "tensor"), P("tensor", "dp")),
        check_vma=False,
    )
```

time: 207 us -> 142 us (0.69)
  Pallas kernels: 0 us -> 92.3 us
  matrix products: 80.9 us -> 2.96 us
  other arithmetic: 36.3 us -> 3.45 us
  blocking collectives: 32.7 us -> 0 us
  local copies, waits for them, and re-layouts: 22.1 us -> 4.25 us
  between operations: 15.9 us -> 2.05 us
  starting transfers between devices: 0.26 us -> 9.6 us
  waiting for transfers between devices: 18.5 us -> 25.9 us
    pallas_call x0 -> x1, Pallas kernels: none -> 92.3 us  [attention(): pl.pallas_call(kernel, grid_spec=pltpu.PrefetchScalarGridSpec(num_scalar_...]
    dot_general x27 -> x1, matrix products: 80.9 us -> 2.96 us  [shards(): projected = jnp.dot(rows, out_weight, preferred_element_type=F32)]
    psum x1 -> x0, blocking collectives: 32.7 us -> none  [shards(): squares = lax.psum(jnp.sum(summed * summed, axis=1), 'dp')]
    reduce_sum x11 -> x1, other arithmetic: 31.6 us -> 0.12 us  [shards(): squares = jnp.sum(summed * summed, axis=1)]
    ppermute x0 -> x9, waiting for transfers between devices: none -> 25.9 us  [swap(): return lax.ppermute(x, axis, [(i, i ^ bit) for i in range(size)])]
    psum x1 -> x0, waiting for transfers between devices: 18.4 us -> none  [shards(): lax.psum(projected.astype(jnp.bfloat16), 'tensor').astype(jnp.float32)]
    slice x2 -> x0, local copies, waits for them, and re-layouts: 11.6 us -> none  [the longest x1 6.4 us: attend(): key_block = cache_keys[:, offset:offset + block_len]]
    ppermute x0 -> x9, starting transfers between devices: none -> 9.6 us  [swap(): return lax.ppermute(x, axis, [(i, i ^ bit) for i in range(size)])]
  transfers between devices with their start and end apart: 2 -> 9, of which waited for: 1 -> 9; matrix products, arithmetic and copies ran while one was open for 50% -> 1% of each run, Pallas kernels for 0% -> 0%
where the time goes in v1:
time: 142 us; the launch traced here: 141 us
  Pallas kernels  92.3 us (65%)
  waiting for transfers between devices  25.9 us (18%)
  starting transfers between devices  9.6 us (7%)
  local copies, waits for them, and re-layouts  4.25 us (3%)
  other arithmetic  3.45 us (2%)
  matrix products  2.96 us (2%)
  between operations  2.05 us (1%)
    pallas_call x1, Pallas kernels, attention(): pl.pallas_call(kernel, grid_spec=pltpu.PrefetchScalarGridSpec(num_scalar_...  92.3 us
    ppermute x9, waiting for transfers between devices, swap(): return lax.ppermute(x, axis, [(i, i ^ bit) for i in range(size)])  25.9 us
    ppermute x9, starting transfers between devices, swap(): return lax.ppermute(x, axis, [(i, i ^ bit) for i in range(size)])  9.6 us
    dot_general x1, matrix products, shards(): projected = jnp.dot(rows, out_weight, preferred_element_type=F32)  2.96 us
  transfers between devices with their start and end apart: 9, of which 9 were waited for; matrix products, arithmetic and copies ran while one was open for 1% of the time, Pallas kernels for 0%

profile of v1, /device:TPU:0, one launch (start us, length us, event | category | flops | bytes accessed | tf_op | source)
XLA Modules:
  0.0 140.5 jit_solution(13418146737498362939)
XLA Ops:
  1.9 2.0 %copy.15 = bf16[32,64,128]{2,1,0:T(8,128)(2,1)} copy(bf16[32,64,128]{2,0,1:T(8,128)(2,1)} %bitcast.29) | data formatting | bytes 1048576 | tf_op jit(solution)/shard_map/transpose | solution.py:188
  4.0 92.3 %attention.1 = (bf16[64,4096]{1,0:T(8,128)(2,1)}, bf16[8,4096]{1,0:T(8,128)(2,1)}) custom-call(s32[1]{0:T(128)S(6)} %copy.20.lens, s32[8]{0:T(128)} %bitcast.32, s32[1]{0:T(128)S(6)} %copy.21.plen, s32[1,64]{1,0:T(1,128)} %parent_ref.1, bf16[4,512,128]{2,1,0:T(8,128)(2,1)} %bitcast.25, bf16[256,128]{1,0:T(8,128)(2,1)} %bitcast.30, ...), custom_call_target="tpu_custom_call" | custom-call | tf_op jit(solution)/shard_map/attention/pallas_call | solution.py:205
  96.3 0.1 collective-permute-start
  96.4 0.9 constant_dynamic-update-slice_fusion.4
  97.3 0.7 gather_fusion
  98.0 3.7 %collective-permute-done = bf16[8,4096]{1,0:T(8,128)(2,1)S(1)} collective-permute-done((bf16[8,4096]{1,0:T(8,128)(2,1)}, bf16[8,4096]{1,0:T(8,128)(2,1)S(1)}, u32[]{:S(2)}, u32[]{:S(2)}) %collective-permute-start) | collective-permute-done | bytes 65568 | tf_op jit(solution)/shard_map/ppermute | solution.py:257
  101.7 0.8 pad_maximum_fusion.2
  102.6 2.8 %collective-permute-start.1 = (bf16[16,4096]{1,0:T(8,128)(2,1)S(1)}, bf16[16,4096]{1,0:T(8,128)(2,1)S(1)}, u32[]{:S(2)}, u32[]{:S(2)}) collective-permute-start(bf16[16,4096]{1,0:T(8,128)(2,1)S(1)} %pad_maximum_fusion.2), channel_id=1, source_target_pairs={{0,8},{2,10},{4,12},{6,14},{8,0},{10,2},{12,4},{14,6},{16,24},{18,... | collective-permute-start | bytes 393224 | tf_op jit(solution)/shard_map/ppermute | solution.py:257
  105.4 2.9 %collective-permute-done.1 = bf16[16,4096]{1,0:T(8,128)(2,1)S(1)} collective-permute-done((bf16[16,4096]{1,0:T(8,128)(2,1)S(1)}, bf16[16,4096]{1,0:T(8,128)(2,1)S(1)}, u32[]{:S(2)}, u32[]{:S(2)}) %collective-permute-start.1) | collective-permute-done | bytes 131104 | tf_op jit(solution)/shard_map/ppermute | solution.py:257
  108.3 0.9 pad_maximum_fusion.1
  109.3 6.3 %collective-permute-done.2 = bf16[32,4096]{1,0:T(8,128)(2,1)S(1)} collective-permute-done((bf16[32,4096]{1,0:T(8,128)(2,1)S(1)}, bf16[32,4096]{1,0:T(8,128)(2,1)S(1)}, u32[]{:S(2)}, u32[]{:S(2)}) %collective-permute-start.2) | collective-permute-done | bytes 262176 | tf_op jit(solution)/shard_map/ppermute | solution.py:257
  115.6 0.9 pad_maximum_fusion
  116.6 1.9 %collective-permute-done.3 = bf16[64,4096]{1,0:T(8,128)(2,1)S(1)} collective-permute-done((bf16[64,4096]{1,0:T(8,128)(2,1)S(1)}, bf16[64,4096]{1,0:T(8,128)(2,1)S(1)}, u32[]{:S(2)}, u32[]{:S(2)}) %collective-permute-start.3) | collective-permute-done | bytes 524320 | tf_op jit(solution)/shard_map/ppermute | solution.py:257
  118.5 3.0 %convolution_bitcast_fusion = f32[16,8,512]{2,1,0:T(8,128)S(1)} fusion(bf16[128,4096]{1,0:T(8,128)(2,1)S(1)} %constant_dynamic-update-slice_fusion, bf16[4096,512]{1,0:T(8,128)(2,1)} %param.21), kind=kOutput, calls=%fused_computation.2 | convolution fusion | flops 536870912 | bytes 5505024 | tf_op jit(solution)/shard_map/dot_general | solution.py:293
  121.5 0.6 gather_fusion.1
  122.1 2.3 %collective-permute-start.4 = (bf16[64,512]{1,0:T(8,128)(2,1)S(1)}, bf16[64,512]{1,0:T(8,128)(2,1)S(1)}, u32[]{:S(2)}, u32[]{:S(2)}) collective-permute-start(bf16[64,512]{1,0:T(8,128)(2,1)S(1)} %dynamic-slice_convert_fusion), channel_id=1, source_target_pairs={{0,1},{1,0},{2,3},{3,2},{4,5},{5,4},{6,7},{7,6},{8,9},{9,8},{10,11... | collective-permute-start | bytes 196616 | tf_op jit(solution)/shard_map/ppermute | solution.py:257
  124.4 2.4 %collective-permute-done.4 = bf16[64,512]{1,0:T(8,128)(2,1)S(1)} collective-permute-done((bf16[64,512]{1,0:T(8,128)(2,1)S(1)}, bf16[64,512]{1,0:T(8,128)(2,1)S(1)}, u32[]{:S(2)}, u32[]{:S(2)}) %collective-permute-start.4) | collective-permute-done | bytes 65568 | tf_op jit(solution)/shard_map/ppermute | solution.py:257
  126.9 2.6 %collective-permute-start.5 = (f32[64]{0:T(128)S(1)}, f32[64]{0:T(128)S(1)}, u32[]{:S(2)}, u32[]{:S(2)}) collective-permute-start(f32[64]{0:T(128)S(1)} %multiply_reduce_fusion), channel_id=1, source_target_pairs={{0,16},{2,18},{4,20},{6,22},{8,24},{10,26},{12,28},{14,30},{16,0},... | collective-permute-start | bytes 776 | tf_op jit(solution)/shard_map/ppermute | solution.py:257
  129.5 2.0 %collective-permute-done.5 = f32[64]{0:T(128)S(1)} collective-permute-done((f32[64]{0:T(128)S(1)}, f32[64]{0:T(128)S(1)}, u32[]{:S(2)}, u32[]{:S(2)}) %collective-permute-start.5) | collective-permute-done | bytes 288 | tf_op jit(solution)/shard_map/ppermute | solution.py:257
  131.5 1.6 %collective-permute-start.6 = (f32[64]{0:T(128)S(1)}, f32[64]{0:T(128)S(1)}, u32[]{:S(2)}, u32[]{:S(2)}) collective-permute-start(f32[64]{0:T(128)S(1)} %add.52), channel_id=1, source_target_pairs={{0,8},{2,10},{4,12},{6,14},{8,0},{10,2},{12,4},{14,6},{16,24},{18,... | collective-permute-start | bytes 776 | tf_op jit(solution)/shard_map/ppermute | solution.py:257
  133.1 2.0 %collective-permute-done.6 = f32[64]{0:T(128)S(1)} collective-permute-done((f32[64]{0:T(128)S(1)}, f32[64]{0:T(128)S(1)}, u32[]{:S(2)}, u32[]{:S(2)}) %collective-permute-start.6) | collective-permute-done | bytes 288 | tf_op jit(solution)/shard_map/ppermute | solution.py:257
  135.0 3.6 %collective-permute-done.7 = f32[64]{0:T(128)S(1)} collective-permute-done((f32[64]{0:T(128)S(1)}, f32[64]{0:T(128)S(1)}, u32[]{:S(2)}, u32[]{:S(2)}) %collective-permute-start.7) | collective-permute-done | bytes 288 | tf_op jit(solution)/shard_map/ppermute | solution.py:257
  138.6 1.2 collective-permute-done.8
  139.8 0.7 multiply_convert_fusion
  (22 shorter events, 0.4 us)
Async XLA Ops:
  4.0 93.3 %copy-start = (s32[16]{0:T(128)S(1)}, s32[16]{0:T(128)}, u32[]{:S(2)}) copy-start(s32[16]{0:T(128)} %constant.28.clone) | copy-start | bytes 196
  96.3 5.4 %collective-permute-start = (bf16[8,4096]{1,0:T(8,128)(2,1)}, bf16[8,4096]{1,0:T(8,128)(2,1)S(1)}, u32[]{:S(2)}, u32[]{:S(2)}) collective-permute-start(bf16[8,4096]{1,0:T(8,128)(2,1)} %get-tuple-element.5), channel_id=1, source_target_pairs={{0,16},{2,18},{4,20},{6,22},{8,24},{10,26},{12,28},{14,30},{16,0},... | collective-permute-start | bytes 196616 | tf_op jit(solution)/shard_map/ppermute | solution.py:257
  102.6 5.7 %collective-permute-start.1 = (bf16[16,4096]{1,0:T(8,128)(2,1)S(1)}, bf16[16,4096]{1,0:T(8,128)(2,1)S(1)}, u32[]{:S(2)}, u32[]{:S(2)}) collective-permute-start(bf16[16,4096]{1,0:T(8,128)(2,1)S(1)} %pad_maximum_fusion.2), channel_id=1, source_target_pairs={{0,8},{2,10},{4,12},{6,14},{8,0},{10,2},{12,4},{14,6},{16,24},{18,... | collective-permute-start | bytes 393224 | tf_op jit(solution)/shard_map/ppermute | solution.py:257
  109.2 6.4 %collective-permute-start.2 = (bf16[32,4096]{1,0:T(8,128)(2,1)S(1)}, bf16[32,4096]{1,0:T(8,128)(2,1)S(1)}, u32[]{:S(2)}, u32[]{:S(2)}) collective-permute-start(bf16[32,4096]{1,0:T(8,128)(2,1)S(1)} %pad_maximum_fusion.1), channel_id=1, source_target_pairs={{0,4},{2,6},{4,0},{6,2},{8,12},{10,14},{12,8},{14,10},{16,20},{18,... | collective-permute-start | bytes 786440 | tf_op jit(solution)/shard_map/ppermute | solution.py:257
  116.5 23.3 %copy-start.1 = (f32[512]{0:T(512)S(1)}, f32[512]{0:T(512)}, u32[]{:S(2)}) copy-start(f32[512]{0:T(512)} %param.22) | copy-start | bytes 6148
  116.5 2.0 %collective-permute-start.3 = (bf16[64,4096]{1,0:T(8,128)(2,1)S(1)}, bf16[64,4096]{1,0:T(8,128)(2,1)S(1)}, u32[]{:S(2)}, u32[]{:S(2)}) collective-permute-start(bf16[64,4096]{1,0:T(8,128)(2,1)S(1)} %pad_maximum_fusion), channel_id=1, source_target_pairs={{0,2},{2,0},{4,6},{6,4},{8,10},{10,8},{12,14},{14,12},{16,18},{18,... | collective-permute-start | bytes 1572872 | tf_op jit(solution)/shard_map/ppermute | solution.py:257
  122.1 4.7 %collective-permute-start.4 = (bf16[64,512]{1,0:T(8,128)(2,1)S(1)}, bf16[64,512]{1,0:T(8,128)(2,1)S(1)}, u32[]{:S(2)}, u32[]{:S(2)}) collective-permute-start(bf16[64,512]{1,0:T(8,128)(2,1)S(1)} %dynamic-slice_convert_fusion), channel_id=1, source_target_pairs={{0,1},{1,0},{2,3},{3,2},{4,5},{5,4},{6,7},{7,6},{8,9},{9,8},{10,11... | collective-permute-start | bytes 196616 | tf_op jit(solution)/shard_map/ppermute | solution.py:257
  126.9 4.5 %collective-permute-start.5 = (f32[64]{0:T(128)S(1)}, f32[64]{0:T(128)S(1)}, u32[]{:S(2)}, u32[]{:S(2)}) collective-permute-start(f32[64]{0:T(128)S(1)} %multiply_reduce_fusion), channel_id=1, source_target_pairs={{0,16},{2,18},{4,20},{6,22},{8,24},{10,26},{12,28},{14,30},{16,0},... | collective-permute-start | bytes 776 | tf_op jit(solution)/shard_map/ppermute | solution.py:257
  131.5 3.6 %collective-permute-start.6 = (f32[64]{0:T(128)S(1)}, f32[64]{0:T(128)S(1)}, u32[]{:S(2)}, u32[]{:S(2)}) collective-permute-start(f32[64]{0:T(128)S(1)} %add.52), channel_id=1, source_target_pairs={{0,8},{2,10},{4,12},{6,14},{8,0},{10,2},{12,4},{14,6},{16,24},{18,... | collective-permute-start | bytes 776 | tf_op jit(solution)/shard_map/ppermute | solution.py:257
  135.0 3.6 %collective-permute-start.7 = (f32[64]{0:T(128)S(1)}, f32[64]{0:T(128)S(1)}, u32[]{:S(2)}, u32[]{:S(2)}) collective-permute-start(f32[64]{0:T(128)S(1)} %add.53), channel_id=1, source_target_pairs={{0,4},{2,6},{4,0},{6,2},{8,12},{10,14},{12,8},{14,10},{16,20},{18,... | collective-permute-start | bytes 776 | tf_op jit(solution)/shard_map/ppermute | solution.py:257
  138.6 1.2 collective-permute-start.8
